TPU v7x, 256 devices: a whole 4x4x8 slice. The times are simulated.
256 devices in a mesh: dp: 2 (over x_lo), context: 8 (over z), tensor: 16 (over y, x_hi, core).
Axes of the slice: x: 4 (x_hi: 2, x_lo: 2; x = x_hi * 2 + x_lo), y: 4, z: 8, core: 2. Of those that a mesh axis runs over, the one named last changes fastest.
Arguments:
- activations: bfloat16 [2, 4096, 4096], P('dp', ('context', 'tensor')), may hold values from -60 to 60
- in_weight: bfloat16 [4096, 3, 4096], P('dp', None, 'tensor'), may hold values from -0.09375 to 0.09375
- out_weight: bfloat16 [4096, 4096], P('tensor', 'dp'), may hold values from -0.09375 to 0.09375
- short_filter: float32 [3, 3, 4096], P(None, None, 'tensor'), may hold values from -2 to 2
- mixer_filter: float32 [128, 256], P(None, 'tensor'), may hold values from -0.5 to 0.5
- cotangent: bfloat16 [2, 4096, 4096], P('dp', ('context', 'tensor')), may hold values from -6 to 6
Outputs:
- block_out: bfloat16 [2, 4096, 4096], P('dp', ('context', 'tensor'))
- grad_input: bfloat16 [2, 4096, 4096], P('dp', ('context', 'tensor'))
- grad_in_weight: bfloat16 [4096, 3, 4096], P(('dp', 'context'), None, 'tensor')
- grad_out_weight: bfloat16 [4096, 4096], P('tensor', ('dp', 'context'))
- grad_short: float32 [3, 3, 4096], P(None, None, 'tensor')
- grad_mixer: float32 [128, 256], P(None, 'tensor')
All inputs are finite; a program needn't handle non-finite values.
Results may differ from a plain program's by a relative error of at most 0.019.
Values may be sent and summed in bfloat16 or wider, within the bound.
A program may use at most 128 MiB of HBM per device.

v0:
```python
import jax
import jax.numpy as jnp
from jax import lax
from jax.sharding import PartitionSpec as P

EPS = 1e-05


def from_behind(value, axis, steps):
    count = lax.axis_size(axis)
    initial, last = (max(0, -steps), min(count, count - steps))
    return lax.ppermute(value, axis, [(source, source + steps) for source in range(initial, last)])


def skew_table(base, span):
    groups = base.shape[0]
    padded = jnp.concatenate([base, jnp.zeros((groups, span + 1), jnp.float32)], axis=1)
    tiled = jnp.tile(padded[:, None, :], (1, span, 1)).reshape(groups, span * (2 * span + 1))
    return tiled[:, : span * 2 * span].reshape(groups, span, 2 * span)


def band_windows(extended, span, groups):
    chans = extended.shape[1]
    padded = jnp.concatenate([extended, jnp.zeros((1, chans), jnp.float32)], 0)
    blocks = padded.shape[0] // span
    padded = padded.reshape(blocks, span, groups, chans // groups)
    return jnp.concatenate([padded[:-1], padded[1:]], axis=1)


def band_apply(table, extended, span):
    groups = table.shape[0]
    chans = extended.shape[1]
    windows = band_windows(extended, span, groups)
    result = jnp.einsum("gtu,bugc->btgc", table, windows, precision=lax.Precision.HIGHEST)
    return result.reshape(windows.shape[0] * span, chans)


def band_grad(left, extended, span, groups):
    rows, chans = left.shape
    lhs = left.reshape(rows // span, span, groups, chans // groups)
    windows = band_windows(extended, span, groups)
    prods = jnp.einsum("btgc,bugc->gtu", lhs, windows, precision=lax.Precision.HIGHEST)
    flat = jnp.concatenate(
        [prods.reshape(groups, span * 2 * span), jnp.zeros((groups, span), jnp.float32)], axis=1
    )
    skewed = flat.reshape(groups, span, 2 * span + 1).sum(axis=1)
    return jnp.flip(skewed[:, :span], axis=1).T


def short_apply(filters, extended, rows):
    taps = filters.shape[1]
    total = jnp.zeros((rows,) + extended.shape[1:], jnp.float32)
    for tap in range(taps):
        total = total + filters[:, tap][None] * extended[taps - 1 - tap : taps - 1 - tap + rows]
    return total


def per_device(activations, in_weight, out_weight, short_filter, mixer_filter, cotangent):
    rows_own = activations.shape[1]
    width = activations.shape[2]
    rows = rows_own * lax.axis_size("tensor")
    span = mixer_filter.shape[0]
    groups = mixer_filter.shape[1]
    taps = short_filter.shape[1]
    chans = short_filter.shape[2]
    own = activations[0].astype(jnp.float32)
    inverse = lax.rsqrt(jnp.mean(own * own, axis=-1, keepdims=True) + EPS)
    normed = (own * inverse).astype(jnp.bfloat16)
    slab = lax.all_gather(normed, "tensor", axis=0, tiled=True)
    full_in, full_out = (
        lax.all_gather(in_weight, "dp", axis=0, tiled=True),
        lax.all_gather(out_weight, "dp", axis=1, tiled=True),
    )
    in_flat = full_in.reshape(width, 3 * chans)
    projected = (
        jnp.dot(slab, in_flat, preferred_element_type=jnp.float32)
        .astype(jnp.bfloat16)
        .reshape(rows, 3, chans)
    )
    proj_wide = projected.astype(jnp.float32)
    table_fwd = skew_table(jnp.flip(mixer_filter, axis=0).T, span)
    table_back = skew_table(mixer_filter.T, span)
    short_rim = from_behind(projected[rows - taps + 1 :], "context", 1)
    proj_ext = jnp.concatenate([short_rim.astype(jnp.float32), proj_wide], 0)
    streams = short_apply(short_filter, proj_ext, rows)
    gated = (streams[:, 1] * streams[:, 2]).astype(jnp.bfloat16)
    gate_rim = from_behind(gated[rows - span + 1 :], "context", 1)
    gate_ext = jnp.concatenate([gate_rim, gated], 0).astype(jnp.float32)
    mixed = band_apply(table_fwd, gate_ext, span)
    output_rows = (streams[:, 0] * mixed).astype(jnp.bfloat16)
    piece = output_rows
    branch = lax.psum_scatter(
        jnp.dot(piece, full_out, preferred_element_type=jnp.float32).astype(jnp.bfloat16),
        "tensor",
        scatter_dimension=0,
        tiled=True,
    ).astype(jnp.float32)
    block_out = (own + branch).astype(jnp.bfloat16)[None]
    cot_slab = lax.all_gather(cotangent[0], "tensor", axis=0, tiled=True)
    grad_rows = lax.dot_general(
        cot_slab, full_out, (((1,), (1,)), ((), ())), preferred_element_type=jnp.float32
    )
    out_term = lax.dot_general(
        output_rows, cot_slab, (((0,), (0,)), ((), ())), preferred_element_type=jnp.float32
    )
    grad_mix = (grad_rows * streams[:, 0]).astype(jnp.bfloat16)
    grad_mix_wide = grad_mix.astype(jnp.float32)
    mix_rim = from_behind(grad_mix[: span - 1], "context", -1)
    grad_gate = band_apply(
        table_back, jnp.concatenate([grad_mix_wide, mix_rim.astype(jnp.float32)], 0), span
    )
    mixer_term = band_grad(grad_mix_wide, gate_ext, span, groups)
    grad_streams = jnp.stack(
        [grad_rows * mixed, grad_gate * streams[:, 2], grad_gate * streams[:, 1]], axis=1
    )
    stream_rim = from_behind(grad_streams[: taps - 1], "context", -1)
    stream_ext = jnp.concatenate([grad_streams, stream_rim], 0)
    grad_proj = jnp.zeros((rows, 3, chans), jnp.float32)
    for tap in range(taps):
        grad_proj = grad_proj + short_filter[:, tap][None] * stream_ext[tap : tap + rows]
    grad_proj = grad_proj.astype(jnp.bfloat16)
    short_terms = [
        jnp.sum(grad_streams * proj_ext[taps - 1 - tap : taps - 1 - tap + rows], axis=0)
        for tap in range(taps)
    ]
    short_term = jnp.stack(short_terms, axis=1)
    grad_short, grad_mixer = lax.psum((short_term, mixer_term), ("dp", "context"))
    proj_flat = grad_proj.reshape(rows, 3 * chans)
    in_term = lax.dot_general(
        slab, proj_flat, (((0,), (0,)), ((), ())), preferred_element_type=jnp.float32
    ).reshape(width, 3, chans)
    grad_in, grad_out = (
        lax.psum_scatter(
            in_term.astype(jnp.bfloat16), ("dp", "context"), scatter_dimension=0, tiled=True
        ).astype(jnp.float32),
        lax.psum_scatter(
            out_term.astype(jnp.bfloat16), ("dp", "context"), scatter_dimension=1, tiled=True
        ).astype(jnp.float32),
    )
    piece = proj_flat
    grad_norm = lax.psum_scatter(
        lax.dot_general(
            piece, in_flat, (((1,), (1,)), ((), ())), preferred_element_type=jnp.float32
        ).astype(jnp.bfloat16),
        "tensor",
        scatter_dimension=0,
        tiled=True,
    ).astype(jnp.float32)
    grad_x = (
        cotangent[0].astype(jnp.float32)
        + inverse * grad_norm
        - own * inverse**3 * jnp.mean(grad_norm * own, axis=-1, keepdims=True)
    )
    grad_input = grad_x.astype(jnp.bfloat16)[None]
    return (
        block_out,
        grad_input,
        grad_in.astype(jnp.bfloat16),
        grad_out.astype(jnp.bfloat16),
        grad_short,
        grad_mixer,
    )


def solution(mesh):
    placed = (
        P("dp", ("context", "tensor"), None),
        P("dp", None, "tensor"),
        P("tensor", "dp"),
        P(None, None, "tensor"),
        P(None, "tensor"),
        P("dp", ("context", "tensor"), None),
    )
    return jax.shard_map(
        per_device,
        mesh=mesh,
        in_specs=placed,
        out_specs=(
            P("dp", ("context", "tensor"), None),
            P("dp", ("context", "tensor"), None),
            P(("dp", "context"), None, "tensor"),
            P("tensor", ("dp", "context")),
            P(None, None, "tensor"),
            P(None, "tensor"),
        ),
        check_vma=False,
    )
```

profile of v0, /device:TPU:8, one launch (start us, length us, event | category | flops | bytes accessed | tf_op | source)
XLA Modules:
  0.0 682.4 jit_solution(12522044125238099399)
XLA Ops:
  10.5 87.6 %all-gather.8.cloned.1.call-done = bf16[4096,3,256]{2,0,1:T(8,128)(2,1)} async-done(((bf16[2048,3,256]{2,0,1:T(8,128)(2,1)}), bf16[4096,3,256]{2,0,1:T(8,128)(2,1)}) %all-gather.8.cloned.1.call-update) | async-done | bytes 6291472 | tf_op jit(solution)/shard_map/all_gather | solution.py:71
  98.1 8.7 %copy.20 = bf16[4096,3,256]{0,2,1:T(8,128)(2,1)} copy(bf16[4096,3,256]{2,0,1:T(8,128)(2,1)} %all-gather.8.cloned.1.call-done) | data formatting | bytes 12582912 | tf_op jit(solution)/shard_map/all_gather | solution.py:71
  106.8 54.3 %all-gather.6.cloned.1.call-done = bf16[512,4096]{1,0:T(8,128)(2,1)} async-done(((bf16[32,4096]{1,0:T(8,128)(2,1)}), bf16[512,4096]{1,0:T(8,128)(2,1)}) %all-gather.6.cloned.1.call-update) | async-done | bytes 4194320 | tf_op jit(solution)/shard_map/all_gather | solution.py:69
  161.1 7.5 %convolution_convert_fusion.3 = bf16[512,768]{1,0:T(8,128)(2,1)S(1)} fusion(bf16[512,4096]{1,0:T(8,128)(2,1)} %all-gather.6.cloned.1.call-done, bf16[4096,768]{0,1:T(8,128)(2,1)} %bitcast.133), kind=kOutput, calls=%fused_computation.27 | convolution fusion | flops 3221618688 | bytes 11272192 | tf_op jit(solution)/shard_map/dot_general | solution.py:76
  168.6 3.5 collective-permute-start
  173.9 26.4 %all-gather.10.cloned.1.call-done = bf16[256,4096]{1,0:T(8,128)(2,1)} async-done(((bf16[256,2048]{1,0:T(8,128)(2,1)}), bf16[256,4096]{1,0:T(8,128)(2,1)}) %all-gather.10.cloned.1.call-update) | async-done | bytes 2097168 | tf_op jit(solution)/shard_map/all_gather | solution.py:72
  200.3 62.2 %all-gather.12.cloned.1.call-done = bf16[1,512,4096]{2,1,0:T(8,128)(2,1)} async-done(((bf16[1,32,4096]{2,1,0:T(8,128)(2,1)}), bf16[1,512,4096]{2,1,0:T(8,128)(2,1)}) %all-gather.12.cloned.1.call-update) | async-done | bytes 4194320 | tf_op jit(solution)/shard_map/all_gather | solution.py:99
  262.5 5.2 fusion.36
  271.8 3.9 tile.17
  283.1 3.9 fusion.15
  289.7 4.7 collective-permute-start.1
  296.4 3.9 tile.15
  306.9 2.1 slice.105
  313.8 2.3 fusion.12
  320.7 4.2 collective-permute-done.3
  327.0 5.1 bitcast_convert_fusion
  333.6 3.3 convolution_convert_fusion.1
  337.0 4.8 convolution_convert_fusion.2
  343.3 8.6 %convolution_convert_fusion = bf16[4096,3,256]{2,0,1:T(8,128)(2,1)} fusion(bf16[512,4096]{1,0:T(8,128)(2,1)} %all-gather.6.cloned.1.call-done, bf16[512,3,256]{0,2,1:T(8,128)(2,1)S(1)} %copy.39), kind=kOutput, calls=%fused_computation.1 | convolution fusion | flops 3224371200 | bytes 11272192 | tf_op jit(solution)/shard_map/dot_general | solution.py:129
  358.9 3.7 reshape.99
  365.1 62.9 %all-reduce.4 = (f32[3,3,256]{2,0,1:T(4,128)S(1)}, f32[128,16]{0,1:T(8,128)}) all-reduce(f32[3,3,256]{2,0,1:T(4,128)S(1)} %pad_maximum_fusion.4, f32[128,16]{0,1:T(8,128)S(1)} %bitcast.141), channel_id=1, replica_groups=mesh['dp'=2,'context'=8,'tensor'=16] {'dp','context'}, use_global_device_ids=true, to_apply=%region_9.10 | all-reduce | flops 4352 | bytes 34816 | tf_op jit(solution)/shard_map/psum | solution.py:127
  429.8 81.3 %reduce-scatter.5.cloned.1.call-done = bf16[32,4096]{1,0:T(8,128)(2,1)} async-done(((bf16[512,4096]{1,0:T(8,128)(2,1)}), bf16[32,4096]{1,0:T(8,128)(2,1)}) %reduce-scatter.5.cloned.1.call-update) | async-done | bytes 262160 | tf_op jit(solution)/shard_map/reduce_scatter | solution.py:92
  513.1 75.3 %reduce-scatter.11.cloned.1.call-done = bf16[256,256]{1,0:T(8,128)(2,1)} async-done(((bf16[256,4096]{1,0:T(8,128)(2,1)}), bf16[256,256]{1,0:T(8,128)(2,1)}) %reduce-scatter.11.cloned.1.call-update) | async-done | bytes 131088 | tf_op jit(solution)/shard_map/reduce_scatter | solution.py:136
  588.4 87.1 %reduce-scatter.9.cloned.1.call-done = bf16[256,3,256]{2,0,1:T(8,128)(2,1)} async-done(((bf16[4096,3,256]{2,0,1:T(8,128)(2,1)}), bf16[256,3,256]{2,0,1:T(8,128)(2,1)}) %reduce-scatter.9.cloned.1.call-update) | async-done | bytes 393232 | tf_op jit(solution)/shard_map/reduce_scatter | solution.py:133
  (140 shorter events, 55.4 us)
Async XLA Ops:
  7.2 90.9 %all-gather.8.cloned.1.call-start = ((), (), s32[]{:S(2)}) async-start(), calls=%async_computation.5 | async-start | bytes 9437184 | tf_op jit(solution)/shard_map/all_gather | solution.py:71
  7.9 2.6 copy-start.20
  7.9 153.2 %all-gather.6.cloned.1.call-start = ((), (), s32[]{:S(2)}) async-start(), calls=%async_computation.4 | async-start | bytes 4456448 | tf_op jit(solution)/shard_map/all_gather | solution.py:69
  9.1 191.1 %all-gather.10.cloned.1.call-start = ((), (), s32[]{:S(2)}) async-start(), calls=%async_computation.6 | async-start | bytes 3145728 | tf_op jit(solution)/shard_map/all_gather | solution.py:72
  9.9 252.6 %all-gather.12.cloned.1.call-start = ((), (), s32[]{:S(2)}) async-start(), calls=%async_computation.11 | async-start | bytes 4456448 | tf_op jit(solution)/shard_map/all_gather | solution.py:99
  10.5 418.2 %reduce-scatter.7.cloned.1.call-start = ((), (), s32[]{:S(2)}) async-start(), calls=%async_computation.8 | async-start | bytes 4456448 | tf_op jit(solution)/shard_map/reduce_scatter | solution.py:141
  168.6 3.8 copy-start.7
  168.6 4.8 collective-permute-start
  173.9 93.9 %copy-start.5 = (f32[512,3,256]{2,0,1:T(8,128)}, f32[512,3,256]{2,0,1:T(8,128)S(1)}, u32[]{:S(2)}) copy-start(f32[512,3,256]{2,0,1:T(8,128)S(1)} %multiply_add_fusion) | copy-start | bytes 4718596
  173.9 96.0 %copy-start.19 = (f32[128,16]{0,1:T(8,128)S(1)}, f32[128,16]{0,1:T(8,128)}, u32[]{:S(2)}) copy-start(f32[128,16]{0,1:T(8,128)} %param.10) | copy-start | bytes 24580
  268.5 11.2 %collective-permute-start.2 = (bf16[127,256]{1,0:T(8,128)(2,1)S(1)}, bf16[127,256]{1,0:T(8,128)(2,1)S(1)}, u32[]{:S(2)}, u32[]{:S(2)}) collective-permute-start(bf16[127,256]{1,0:T(8,128)(2,1)S(1)} %slice.125), channel_id=1, source_target_pairs={{16,0},{32,16},{48,32},{64,48},{80,64},{96,80},{112,96},{17,1},{33... | collective-permute-start | bytes 195080 | tf_op jit(solution)/shard_map/ppermute | solution.py:12
  277.2 2.0 copy-start.14
  289.7 14.2 %collective-permute-start.1 = (bf16[127,256]{1,0:T(8,128)(2,1)S(1)}, bf16[127,256]{1,0:T(8,128)(2,1)S(1)}, u32[]{:S(2)}, u32[]{:S(2)}) collective-permute-start(bf16[127,256]{1,0:T(8,128)(2,1)S(1)} %slice_bitcast_fusion.1), channel_id=1, source_target_pairs={{0,16},{16,32},{32,48},{48,64},{64,80},{80,96},{96,112},{1,17},{17... | collective-permute-start | bytes 195080 | tf_op jit(solution)/shard_map/ppermute | solution.py:12
  301.9 2.0 copy-start.17
  310.0 3.3 copy-start.12
  313.4 2.7 copy-start.1
  317.4 9.6 %slice-start.2 = ((s8[6291456]{0:T(1024)(128)(4,1)}), s8[4194304]{0:T(1024)(128)(4,1)S(1)}, s32[]{:S(2)}) async-start(s8[6291456]{0:T(1024)(128)(4,1)} %bitcast.131), calls=%async_computation.14 | async-start | bytes 8388608
  319.1 7.8 %slice-start.3 = ((s8[6291456]{0:T(1024)(128)(4,1)}), s8[2097152]{0:T(1024)(128)(4,1)S(1)}, s32[]{:S(2)}) async-start(s8[6291456]{0:T(1024)(128)(4,1)} %bitcast.131), calls=%async_computation.15 | async-start | bytes 4194304
  319.1 5.8 collective-permute-start.3
  332.1 179.0 %reduce-scatter.5.cloned.1.call-start = ((), (), s32[]{:S(2)}) async-start(), calls=%async_computation.7 | async-start | bytes 4456448 | tf_op jit(solution)/shard_map/reduce_scatter | solution.py:92
  336.9 251.5 %reduce-scatter.11.cloned.1.call-start = ((), (), s32[]{:S(2)}) async-start(), calls=%async_computation.10 | async-start | bytes 2228224 | tf_op jit(solution)/shard_map/reduce_scatter | solution.py:136
  341.8 333.7 %reduce-scatter.9.cloned.1.call-start = ((), (), s32[]{:S(2)}) async-start(), calls=%async_computation.9 | async-start | bytes 6684672 | tf_op jit(solution)/shard_map/reduce_scatter | solution.py:133
  362.8 2.0 copy-start.8
  364.8 146.2 %copy-start.18 = (bf16[1,32,4096]{2,1,0:T(8,128)(2,1)S(1)}, bf16[1,32,4096]{2,1,0:T(8,128)(2,1)}, u32[]{:S(2)}) copy-start(bf16[1,32,4096]{2,1,0:T(8,128)(2,1)} %param.11) | copy-start | bytes 786436
  (13 other events, 16.8 us)
Sparse Core Ops, SparseCore 0:
  9.8 88.2 all-gather.7
  101.4 59.5 all-gather.5
  162.9 37.3 all-gather.9
  202.9 59.5 all-gather.11
  332.2 87.3 reduce-scatter.6
  423.8 87.2 reduce-scatter.4
  514.1 74.2 reduce-scatter.10
  591.5 83.9 reduce-scatter.8
where the time goes:
time: 683 us; the launch traced here: 682 us
  waiting for transfers between devices  481 us (70%)
  blocking collectives  62.9 us (9%)
  local copies, waits for them, and re-layouts  60.3 us (9%)
  matrix products  41.7 us (6%)
  between operations  14.6 us (2%)
  starting transfers between devices  11.6 us (2%)
  other arithmetic  10.4 us (2%)
    all_gather x1, waiting for transfers between devices, per_device(): lax.all_gather(in_weight, 'dp', axis=0, tiled=True)  87.6 us
    reduce_scatter x1, waiting for transfers between devices, per_device(): lax.psum_scatter(in_term.astype(jnp.bfloat16), ('dp', 'context'), scatter...  87.1 us
    reduce_scatter x1, waiting for transfers between devices, per_device(): lax.psum_scatter(jnp.dot(piece, full_out, preferred_element_type=jnp.floa...  81.3 us
    reduce_scatter x1, waiting for transfers between devices, per_device(): lax.psum_scatter(out_term.astype(jnp.bfloat16), ('dp', 'context'), scatte...  75.3 us
    psum x1, blocking collectives, per_device(): lax.psum((short_term, mixer_term), ('dp', 'context'))  62.9 us
    all_gather x1, waiting for transfers between devices, per_device(): cot_slab = lax.all_gather(cotangent[0], 'tensor', axis=0, tiled=True)  62.2 us
    all_gather x1, waiting for transfers between devices, per_device(): slab = lax.all_gather(normed, 'tensor', axis=0, tiled=True)  54.3 us
    all_gather x1, waiting for transfers between devices, per_device(): lax.all_gather(out_weight, 'dp', axis=1, tiled=True)  26.4 us
  transfers between devices with their start and end apart: 12, of which 9 were waited for; matrix products, arithmetic and copies ran while one was open for 10% of the time, Pallas kernels for 0%

commit v1 on v0

--- a/solution.py
+++ b/solution.py
@@ -66,7 +66,9 @@
     own = activations[0].astype(jnp.float32)
     inverse = lax.rsqrt(jnp.mean(own * own, axis=-1, keepdims=True) + EPS)
     normed = (own * inverse).astype(jnp.bfloat16)
-    slab = lax.all_gather(normed, "tensor", axis=0, tiled=True)
+    slab = jnp.concatenate(
+        lax.all_to_all(jnp.stack([normed] * lax.axis_size("tensor")), "tensor", 0, 0), axis=0
+    )
     full_in, full_out = (
         lax.all_gather(in_weight, "dp", axis=0, tiled=True),
         lax.all_gather(out_weight, "dp", axis=1, tiled=True),

time: 683 us -> 661 us (0.968)
  waiting for transfers between devices: 481 us -> 449 us
  starting transfers between devices: 11.6 us -> 19.4 us
    all_gather x1 -> x0, waiting for transfers between devices: 54.3 us -> none  [per_device(): slab = lax.all_gather(normed, 'tensor', axis=0, tiled=True)]
    all_gather x1, waiting for transfers between devices: 87.6 us -> 114 us  [per_device(): lax.all_gather(in_weight, 'dp', axis=0, tiled=True)]
    all_to_all x0 -> x1, starting transfers between devices: none -> 7.52 us  [per_device(): lax.all_to_all(jnp.stack([normed] * lax.axis_size('tensor')), 'tensor', 0...]
  transfers between devices with their start and end apart: 12 -> 12, of which waited for: 9 -> 8; matrix products, arithmetic and copies ran while one was open for 10% -> 10% of each run, Pallas kernels for 0% -> 0%
where the time goes in v1:
time: 661 us; the launch traced here: 659 us
  waiting for transfers between devices  449 us (68%)
  blocking collectives  62.9 us (10%)
  local copies, waits for them, and re-layouts  62.6 us (9%)
  matrix products  41.6 us (6%)
  starting transfers between devices  19.4 us (3%)
  between operations  14.6 us (2%)
  other arithmetic  9.66 us (1%)
    all_gather x1, waiting for transfers between devices, per_device(): lax.all_gather(in_weight, 'dp', axis=0, tiled=True)  114 us
    reduce_scatter x1, waiting for transfers between devices, per_device(): lax.psum_scatter(in_term.astype(jnp.bfloat16), ('dp', 'context'), scatter...  87.3 us
    reduce_scatter x1, waiting for transfers between devices, per_device(): lax.psum_scatter(jnp.dot(piece, full_out, preferred_element_type=jnp.floa...  81.3 us
    reduce_scatter x1, waiting for transfers between devices, per_device(): lax.psum_scatter(out_term.astype(jnp.bfloat16), ('dp', 'context'), scatte...  75.3 us
    psum x1, blocking collectives, per_device(): lax.psum((short_term, mixer_term), ('dp', 'context'))  62.9 us
    all_gather x1, waiting for transfers between devices, per_device(): cot_slab = lax.all_gather(cotangent[0], 'tensor', axis=0, tiled=True)  62.4 us
    all_gather x1, waiting for transfers between devices, per_device(): lax.all_gather(out_weight, 'dp', axis=1, tiled=True)  21.5 us
    unnamed x54, local copies, waits for them, and re-layouts  13.9 us
  transfers between devices with their start and end apart: 12, of which 8 were waited for; matrix products, arithmetic and copies ran while one was open for 10% of the time, Pallas kernels for 0%

profile of v1, /device:TPU:8, one launch (start us, length us, event | category | flops | bytes accessed | tf_op | source)
XLA Modules:
  0.0 659.5 jit_solution(5653169715225890364)
XLA Ops:
  9.7 2.5 stack.19
  12.2 7.5 %all-to-all-start = ((bf16[16,32,4096]{2,1,0:T(8,128)(2,1)}), bf16[16,32,4096]{2,1,0:T(8,128)(2,1)}, u32[]{:S(2)}, u32[]{:S(2)}) async-start(bf16[16,32,4096]{2,1,0:T(8,128)(2,1)} %stack.19), calls=%async_computation | async-start | bytes 8388608 | tf_op jit(solution)/shard_map/all_to_all | solution.py:70
  19.8 114.3 %all-gather.5.cloned.1.call-done = bf16[4096,3,256]{2,0,1:T(8,128)(2,1)} async-done(((bf16[2048,3,256]{2,0,1:T(8,128)(2,1)}), bf16[4096,3,256]{2,0,1:T(8,128)(2,1)}) %all-gather.5.cloned.1.call-update) | async-done | bytes 6291472 | tf_op jit(solution)/shard_map/all_gather | solution.py:73
  134.1 8.7 %copy.21 = bf16[4096,3,256]{0,2,1:T(8,128)(2,1)} copy(bf16[4096,3,256]{2,0,1:T(8,128)(2,1)} %all-gather.5.cloned.1.call-done) | data formatting | bytes 12582912 | tf_op jit(solution)/shard_map/all_gather | solution.py:73
  142.8 7.5 %convolution_convert_fusion.3 = bf16[512,768]{1,0:T(8,128)(2,1)S(1)} fusion(bf16[512,4096]{1,0:T(8,128)(2,1)} %bitcast.2, bf16[4096,768]{0,1:T(8,128)(2,1)} %bitcast.153), kind=kOutput, calls=%fused_computation.26 | convolution fusion | flops 3221618688 | bytes 11272192 | tf_op jit(solution)/shard_map/dot_general | solution.py:78
  150.4 3.8 collective-permute-start
  156.0 21.5 %all-gather.7.cloned.1.call-done = bf16[256,4096]{1,0:T(8,128)(2,1)} async-done(((bf16[256,2048]{1,0:T(8,128)(2,1)}), bf16[256,4096]{1,0:T(8,128)(2,1)}) %all-gather.7.cloned.1.call-update) | async-done | bytes 2097168 | tf_op jit(solution)/shard_map/all_gather | solution.py:74
  177.4 62.4 %all-gather.9.cloned.1.call-done = bf16[1,512,4096]{2,1,0:T(8,128)(2,1)} async-done(((bf16[1,32,4096]{2,1,0:T(8,128)(2,1)}), bf16[1,512,4096]{2,1,0:T(8,128)(2,1)}) %all-gather.9.cloned.1.call-update) | async-done | bytes 4194320 | tf_op jit(solution)/shard_map/all_gather | solution.py:101
  239.8 5.2 fusion.40
  249.2 3.9 tile.17
  260.5 3.9 fusion.14
  267.1 4.6 collective-permute-start.1
  273.6 3.9 tile.15
  290.9 2.3 fusion.11
  298.0 4.0 collective-permute-done.3
  304.0 5.0 bitcast_convert_fusion
  310.6 3.3 convolution_convert_fusion.1
  314.0 4.8 convolution_convert_fusion.2
  320.2 8.6 %convolution_convert_fusion = bf16[4096,3,256]{2,0,1:T(8,128)(2,1)} fusion(bf16[512,4096,1]{1,0,2:T(8,128)(2,1)} %bitcast.21, bf16[512,3,256]{0,2,1:T(8,128)(2,1)S(1)} %copy.40), kind=kOutput, calls=%fused_computation.1 | convolution fusion | flops 3224371200 | bytes 11272192 | tf_op jit(solution)/shard_map/dot_general | solution.py:131
  335.9 3.7 reshape.111
  342.1 62.9 %all-reduce.4 = (f32[3,3,256]{2,0,1:T(4,128)S(1)}, f32[128,16]{0,1:T(8,128)}) all-reduce(f32[3,3,256]{2,0,1:T(4,128)S(1)} %pad_maximum_fusion.4, f32[128,16]{0,1:T(8,128)S(1)} %bitcast.161), channel_id=1, replica_groups=mesh['dp'=2,'context'=8,'tensor'=16] {'dp','context'}, use_global_device_ids=true, to_apply=%region_9.10 | all-reduce | flops 4352 | bytes 34816 | tf_op jit(solution)/shard_map/psum | solution.py:129
  406.8 81.3 %reduce-scatter.5.cloned.1.call-done = bf16[32,4096]{1,0:T(8,128)(2,1)} async-done(((bf16[512,4096]{1,0:T(8,128)(2,1)}), bf16[32,4096]{1,0:T(8,128)(2,1)}) %reduce-scatter.5.cloned.1.call-update) | async-done | bytes 262160 | tf_op jit(solution)/shard_map/reduce_scatter | solution.py:94
  490.1 75.3 %reduce-scatter.11.cloned.1.call-done = bf16[256,256]{1,0:T(8,128)(2,1)} async-done(((bf16[256,4096]{1,0:T(8,128)(2,1)}), bf16[256,256]{1,0:T(8,128)(2,1)}) %reduce-scatter.11.cloned.1.call-update) | async-done | bytes 131088 | tf_op jit(solution)/shard_map/reduce_scatter | solution.py:138
  565.4 87.3 %reduce-scatter.9.cloned.1.call-done = bf16[256,3,256]{2,0,1:T(8,128)(2,1)} async-done(((bf16[4096,3,256]{2,0,1:T(8,128)(2,1)}), bf16[256,3,256]{2,0,1:T(8,128)(2,1)}) %reduce-scatter.9.cloned.1.call-update) | async-done | bytes 393232 | tf_op jit(solution)/shard_map/reduce_scatter | solution.py:135
  (140 shorter events, 56.8 us)
Async XLA Ops:
  7.2 2.2 copy-start.6
  7.2 127.0 %all-gather.5.cloned.1.call-start = ((), (), s32[]{:S(2)}) async-start(), calls=%async_computation.5 | async-start | bytes 9437184 | tf_op jit(solution)/shard_map/all_gather | solution.py:73
  7.9 169.5 %all-gather.7.cloned.1.call-start = ((), (), s32[]{:S(2)}) async-start(), calls=%async_computation.6 | async-start | bytes 3145728 | tf_op jit(solution)/shard_map/all_gather | solution.py:74
  8.7 231.2 %all-gather.9.cloned.1.call-start = ((), (), s32[]{:S(2)}) async-start(), calls=%async_computation.11 | async-start | bytes 4456448 | tf_op jit(solution)/shard_map/all_gather | solution.py:101
  12.2 7.6 %copy-start.20 = (f32[3,3,256]{2,1,0:T(4,128)S(1)}, f32[3,3,256]{2,1,0:T(4,128)}, u32[]{:S(2)}) copy-start(f32[3,3,256]{2,1,0:T(4,128)} %param.9) | copy-start | bytes 27652
  12.2 130.6 %all-to-all-start = ((bf16[16,32,4096]{2,1,0:T(8,128)(2,1)}), bf16[16,32,4096]{2,1,0:T(8,128)(2,1)}, u32[]{:S(2)}, u32[]{:S(2)}) async-start(bf16[16,32,4096]{2,1,0:T(8,128)(2,1)} %stack.19), calls=%async_computation | async-start | bytes 8388608 | tf_op jit(solution)/shard_map/all_to_all | solution.py:70
  19.8 385.9 %reduce-scatter.7.cloned.1.call-start = ((), (), s32[]{:S(2)}) async-start(), calls=%async_computation.8 | async-start | bytes 4456448 | tf_op jit(solution)/shard_map/reduce_scatter | solution.py:143
  150.3 4.2 copy-start.7
  150.4 5.1 collective-permute-start
  156.0 89.1 %copy-start.5 = (f32[512,3,256]{2,0,1:T(8,128)}, f32[512,3,256]{2,0,1:T(8,128)S(1)}, u32[]{:S(2)}) copy-start(f32[512,3,256]{2,0,1:T(8,128)S(1)} %multiply_add_fusion) | copy-start | bytes 4718596
  156.0 91.4 %copy-start.19 = (f32[128,16]{0,1:T(8,128)S(1)}, f32[128,16]{0,1:T(8,128)}, u32[]{:S(2)}) copy-start(f32[128,16]{0,1:T(8,128)} %param.10) | copy-start | bytes 24580
  245.8 11.3 %collective-permute-start.2 = (bf16[127,256]{1,0:T(8,128)(2,1)S(1)}, bf16[127,256]{1,0:T(8,128)(2,1)S(1)}, u32[]{:S(2)}, u32[]{:S(2)}) collective-permute-start(bf16[127,256]{1,0:T(8,128)(2,1)S(1)} %slice.125), channel_id=1, source_target_pairs={{16,0},{32,16},{48,32},{64,48},{80,64},{96,80},{112,96},{17,1},{33... | collective-permute-start | bytes 195080 | tf_op jit(solution)/shard_map/ppermute | solution.py:12
  267.1 14.0 %collective-permute-start.1 = (bf16[127,256]{1,0:T(8,128)(2,1)S(1)}, bf16[127,256]{1,0:T(8,128)(2,1)S(1)}, u32[]{:S(2)}, u32[]{:S(2)}) collective-permute-start(bf16[127,256]{1,0:T(8,128)(2,1)S(1)} %slice_bitcast_fusion.1), channel_id=1, source_target_pairs={{0,16},{16,32},{32,48},{48,64},{64,80},{80,96},{96,112},{1,17},{17... | collective-permute-start | bytes 195080 | tf_op jit(solution)/shard_map/ppermute | solution.py:12
  279.1 2.0 copy-start.17
  287.1 3.3 copy-start.12
  290.5 2.7 copy-start.1
  294.5 9.5 %slice-start.2 = ((s8[6291456]{0:T(1024)(128)(4,1)}), s8[4194304]{0:T(1024)(128)(4,1)S(1)}, s32[]{:S(2)}) async-start(s8[6291456]{0:T(1024)(128)(4,1)} %bitcast.151), calls=%async_computation.14 | async-start | bytes 8388608
  296.2 7.8 %slice-start.3 = ((s8[6291456]{0:T(1024)(128)(4,1)}), s8[2097152]{0:T(1024)(128)(4,1)S(1)}, s32[]{:S(2)}) async-start(s8[6291456]{0:T(1024)(128)(4,1)} %bitcast.151), calls=%async_computation.15 | async-start | bytes 4194304
  296.2 5.8 collective-permute-start.3
  309.1 179.0 %reduce-scatter.5.cloned.1.call-start = ((), (), s32[]{:S(2)}) async-start(), calls=%async_computation.7 | async-start | bytes 4456448 | tf_op jit(solution)/shard_map/reduce_scatter | solution.py:94
  313.9 251.4 %reduce-scatter.11.cloned.1.call-start = ((), (), s32[]{:S(2)}) async-start(), calls=%async_computation.10 | async-start | bytes 2228224 | tf_op jit(solution)/shard_map/reduce_scatter | solution.py:138
  318.8 333.8 %reduce-scatter.9.cloned.1.call-start = ((), (), s32[]{:S(2)}) async-start(), calls=%async_computation.9 | async-start | bytes 6684672 | tf_op jit(solution)/shard_map/reduce_scatter | solution.py:135
  339.8 2.0 copy-start.8
  341.8 146.2 %copy-start.18 = (bf16[1,32,4096]{2,1,0:T(8,128)(2,1)S(1)}, bf16[1,32,4096]{2,1,0:T(8,128)(2,1)}, u32[]{:S(2)}) copy-start(bf16[1,32,4096]{2,1,0:T(8,128)(2,1)} %param.11) | copy-start | bytes 786436
  (13 other events, 18.1 us)
Sparse Core Ops, SparseCore 0:
  9.8 124.3 all-gather.4
  135.9 41.4 all-gather.6
  180.2 59.5 all-gather.8
  309.2 87.4 reduce-scatter.6
  400.8 87.2 reduce-scatter.4
  491.0 74.3 reduce-scatter.10
  568.5 84.0 reduce-scatter.8
